TPU v7x, 32 devices: a whole 2x2x4 slice. The times are simulated.
32 devices in a mesh: seg: 16 (over z, y, x), dir: 2 (over core).
Axes of the slice: x: 2, y: 2, z: 4, core: 2. Of those that a mesh axis runs over, the one named last changes fastest.
Arguments:
- strain: float32 [128, 8, 6, 8192], P('seg'), may hold values from -6 to 6
- valid_flags: int32 [128, 8], P('seg'), may hold values from 0 to 1, as said below
- direction_ids: int32 [1024], P('dir'), may hold values from 0 to 3071
- grid_patterns: float32 [3072, 6], replicated, may hold values from -1 to 1
- grid_delays: float32 [3072, 3], replicated, may hold values from -40 to 40
Outputs:
- peak: float32 [8, 8192], P(None, 'seg')
- dir_score: float32 [8, 1024], P(None, 'dir')
Inputs may be any that keep to these rules, and one draw needn't show every extreme that they name: `valid_flags`: in every draw one window has no usable segment.
All inputs are finite; a program needn't handle non-finite values.
Results may differ from a plain program's by a relative error of at most 0.0001.
Values sent between devices are 32-bit elements; how exact they have to be, the bound alone decides.
No kernel may reach another device: no remote copies, remote signals or barrier semaphores. Data moves between devices by JAX's collectives and lax.ppermute only.
A program may use at most 64 MiB of HBM per device.

v0:
```python
import math

import jax
import jax.numpy as jnp
from jax import lax
from jax.sharding import PartitionSpec as P

F = 8192


PAIRS = ((0, 1), (0, 2), (1, 2))


def spectra(strain, valid_flags):
    weight = valid_flags.astype(jnp.float32)[:, :, None]
    real_part = strain[:, :, 0:3, :]
    imag_part = strain[:, :, 3:6, :]
    parts = []
    for d in range(3):
        parts.append(
            jnp.sum(
                weight
                * (
                    real_part[:, :, d] * real_part[:, :, d]
                    + imag_part[:, :, d] * imag_part[:, :, d]
                ),
                0,
            )
        )
    for d, e in PAIRS:
        parts.append(
            jnp.sum(
                weight
                * (
                    real_part[:, :, d] * real_part[:, :, e]
                    + imag_part[:, :, d] * imag_part[:, :, e]
                ),
                0,
            )
        )
    for d, e in PAIRS:
        parts.append(
            jnp.sum(
                weight
                * (
                    imag_part[:, :, d] * real_part[:, :, e]
                    - real_part[:, :, d] * imag_part[:, :, e]
                ),
                0,
            )
        )
    return jnp.stack(parts, 0)


def null_vectors(rows):
    plus = rows[:, 0:3]
    cross = rows[:, 3:6]
    first = plus[:, 1] * cross[:, 2] - plus[:, 2] * cross[:, 1]
    second = plus[:, 2] * cross[:, 0] - plus[:, 0] * cross[:, 2]
    third = plus[:, 0] * cross[:, 1] - plus[:, 1] * cross[:, 0]
    null = jnp.stack([first, second, third], 1)
    norm2 = jnp.maximum(jnp.sum(null * null, 1), 0.25)
    return (null, norm2)


def project(cov, first_bin, null, norm2, delays, count, total_bins):
    width = cov.shape[2]
    freq = (first_bin + jnp.arange(width, dtype=jnp.int32)).astype(jnp.float32) * (
        2.0 * math.pi / total_bins
    )
    energy = jnp.zeros((null.shape[0], cov.shape[1], width), jnp.float32)
    for d in range(3):
        energy = energy + (null[:, d] * null[:, d])[:, None, None] * cov[d][None]
    for index, (d, e) in enumerate(PAIRS):
        angle = (delays[:, d] - delays[:, e])[:, None] * freq[None, :]
        factor = (2.0 * null[:, d] * null[:, e])[:, None, None]
        energy = energy + factor * (
            jnp.cos(angle)[:, None, :] * cov[3 + index][None]
            + jnp.sin(angle)[:, None, :] * cov[6 + index][None]
        )
    return energy / (norm2[:, None, None] * jnp.maximum(count, 1.0)[None, :, None])


def shards(strain, valid_flags, direction_ids, grid_patterns, grid_delays):
    grid_points = grid_patterns.shape[0]
    one_hot = (direction_ids[:, None] == jnp.arange(grid_points, dtype=jnp.int32)[None, :]).astype(
        jnp.float32
    )
    table = jnp.concatenate([grid_patterns, grid_delays], 1)
    picked = jnp.dot(
        one_hot, table, precision=lax.Precision.HIGHEST, preferred_element_type=jnp.float32
    )
    null, norm2 = null_vectors(picked[:, 0:6])
    delays = picked[:, 6:9]
    count_part = jnp.sum(valid_flags.astype(jnp.float32), 0)
    bin_share = F // lax.axis_size("seg")
    first_bin = lax.axis_index("seg") * bin_share
    cov = lax.psum_scatter(spectra(strain, valid_flags), "seg", scatter_dimension=2, tiled=True)
    count = lax.psum(count_part, "seg")
    power = project(cov, first_bin, null, norm2, delays, count, F)
    peak_part = jnp.max(power, 0)
    score = lax.psum(jnp.sum(power, 2) / F, "seg")
    peak = lax.pmax(peak_part, "dir")
    return (peak, score.T)


def solution(mesh):
    placed = (P("seg", None, None, None), P("seg", None), P("dir"), P(), P())
    return jax.shard_map(
        shards,
        mesh=mesh,
        in_specs=placed,
        out_specs=(P(None, "seg"), P(None, "dir")),
        check_vma=False,
    )
```

profile of v0, /device:TPU:0, one launch (start us, length us, event | category | flops | bytes accessed | tf_op | source)
XLA Modules:
  0.0 199.6 jit_solution(11500045621607774981)
XLA Ops:
  7.2 0.0 reduce-scatter.2.cloned.1.call-start
  7.2 0.7 convert_element_type.12
  7.9 6.5 %fusion.34 = (f32[8,8192]{1,0:T(8,128)S(1)}, f32[8,8192]{1,0:T(8,128)S(1)}, f32[8,8192]{1,0:T(8,128)S(1)}, f32[8,8192]{1,0:T(8,128)S(1)}, f32[8,8192]{1,0:T(8,12...) fusion(f32[8,8,6,8192]{3,1,2,0:T(8,128)} %param.5, ...), kind=kLoop, calls=%fused_computation.48 | loop fusion | flops 23003136 | bytes 14942464 | tf_op jit(solution)/shard_map/reduce_sum | solution.py:43
  14.5 0.0 copy-start.1
  14.5 0.0 copy-start.2
  14.5 0.0 copy-start.3
  14.6 0.0 copy-start.4
  14.7 0.0 copy-start
  14.7 1.4 copy-done
  16.1 0.0 reduce-scatter.2.cloned.1.call-update
  16.1 0.0 copy-done.1
  16.2 43.8 %psum.14 = f32[8]{0:T(128)S(1)} all-reduce(f32[8]{0:T(128)S(1)} %convert_reduce_fusion), channel_id=1, replica_groups=mesh['seg'=16,'dir'=2] {'seg'}, use_global_device_ids=true, to_apply=%region_12.0 | all-reduce | flops 8 | bytes 64 | tf_op jit(solution)/shard_map/psum | solution.py:99
  60.0 0.0 copy-done.2
  60.0 0.0 copy-done.3
  60.0 0.0 copy-done.4
  60.0 3.0 %fusion = f32[512,9]{0,1:T(8,128)S(1)} fusion(s32[512]{0:T(512)S(1)} %copy-done.4, f32[3072,3]{0,1:T(4,128)S(1)} %copy-done.3, f32[3072,6]{0,1:T(8,128)S(1)} %copy-done.2), kind=kOutput, calls=%fused_computation.2 | convolution fusion | flops 171469824 | bytes 131072 | tf_op jit(solution)/shard_map/dot_general | solution.py:90
  63.0 0.1 slice_subtract_fusion.2
  63.1 0.1 broadcast_multiply_fusion
  63.2 12.5 %multiply_cosine_fusion.2 = (f32[512,512]{1,0:T(8,128)S(1)}, f32[512,512]{1,0:T(8,128)S(1)}, f32[512,512]{1,0:T(8,128)S(1)}, f32[512,512]{1,0:T(8,128)}, f32[512,512]{1,0:T(8,128)}, /*index=5*/f32[512,512]{1,0:T(8,128)}) fusion(f32[512]{0:T(512)S(1)} %convert_multiply_fusion, f32[512]{0:T(512)S(1)} %bitcast.242, f32[512]{0:T(512)S(1)} %bitcast.243, ...), kind=kLoop, calls=%fused_computation.63 | loop fusion | flops 786432 | bytes 6299648 | tf_op jit(solution)/shard_map/cos | solution.py:78
  75.7 25.3 %reduce-scatter.2.cloned.1.call-done = f32[9,8,512]{2,1,0:T(8,128)} async-done(((f32[9,8,8192]{2,1,0:T(8,128)}), f32[9,8,512]{2,1,0:T(8,128)}) %reduce-scatter.2.cloned.1.call-update) | async-done | bytes 147472 | tf_op jit(solution)/shard_map/reduce_scatter | solution.py:98
  101.0 0.9 slice_bitcast_fusion.8
  101.9 10.6 %fusion.44 = (f32[512,8]{1,0:T(8,128)S(1)}, f32[8,512]{1,0:T(8,128)S(1)}) fusion(f32[512,8]{1,0:T(8,128)S(1)} %broadcast_multiply_fusion, f32[8,512]{1,0:T(8,128)S(1)} %get-tuple-element.23, f32[512,512]{1,0:T(8,128)} %get-tuple-element.51, f32[8,512]{1,0:T(8,128)S(1)} %get-tuple-element.24, f32[512,512]{1,0:T(8,128)} %get-tuple-element.52, ...), kind=kLoop, calls=%fused_computation.102 | loop fusion | flops 48226304 | bytes 6500352 | tf_op jit(solution)/shard_map/reduce_sum | solution.py:102
  112.5 75.6 %psum.15 = f32[8,512]{0,1:T(8,128)S(1)} all-reduce(f32[8,512]{0,1:T(8,128)S(1)} %multiply_bitcast_fusion), channel_id=1, replica_groups=mesh['seg'=16,'dir'=2] {'seg'}, use_global_device_ids=true, to_apply=%region_16.0 | all-reduce | flops 4096 | bytes 32768 | tf_op jit(solution)/shard_map/psum | solution.py:102
  188.1 0.7 copy.31
  188.8 3.9 %pmax.7 = f32[8,512]{1,0:T(8,128)} all-reduce(f32[8,512]{1,0:T(8,128)S(1)} %get-tuple-element.14), channel_id=1, replica_groups=mesh['seg'=16,'dir'=2] {'dir'}, use_global_device_ids=true, to_apply=%region_14.0 | all-reduce | flops 4096 | bytes 32768 | tf_op jit(solution)/shard_map/pmax | solution.py:103
  (17 shorter events, 0.3 us)
Async XLA Ops:
  7.2 93.9 %reduce-scatter.2.cloned.1.call-start = ((), (), s32[]{:S(2)}) async-start(), calls=%async_computation.1 | async-start | bytes 2506752 | tf_op jit(solution)/shard_map/reduce_scatter | solution.py:98
  14.5 1.6 copy-start.1
  14.5 45.4 %copy-start.2 = (f32[3072,6]{0,1:T(8,128)S(1)}, f32[3072,6]{0,1:T(8,128)}, u32[]{:S(2)}) copy-start(f32[3072,6]{0,1:T(8,128)} %param.8) | copy-start | bytes 221188
  14.5 45.4 %copy-start.3 = (f32[3072,3]{0,1:T(4,128)S(1)}, f32[3072,3]{0,1:T(4,128)}, u32[]{:S(2)}) copy-start(f32[3072,3]{0,1:T(4,128)} %param.9) | copy-start | bytes 110596
  14.6 45.4 %copy-start.4 = (s32[512]{0:T(512)S(1)}, s32[512]{0:T(512)}, u32[]{:S(2)}) copy-start(s32[512]{0:T(512)} %param.7) | copy-start | bytes 6148
  14.7 1.4 copy-start
Sparse Core Ops, SparseCore 0:
  16.2 84.7 reduce-scatter.1
where the time goes:
time: 200 us
  blocking collectives  123 us (62%)
  other arithmetic  30.5 us (15%)
  waiting for transfers between devices  25.3 us (13%)
  between operations  14.2 us (7%)
  local copies, waits for them, and re-layouts  3.19 us (2%)
  matrix products  2.97 us (1%)
    psum x1, blocking collectives, shards(): score = lax.psum(jnp.sum(power, 2) / F, 'seg')  75.6 us
    psum x1, blocking collectives, shards(): count = lax.psum(count_part, 'seg')  43.8 us
    reduce_scatter x1, waiting for transfers between devices, shards(): lax.psum_scatter(spectra(strain, valid_flags), 'seg', scatter_dimension=2...  25.3 us
    cos x1, other arithmetic, project(): jnp.cos(angle)[:, None, :] * cov[3 + index][None]  12.5 us
    reduce_sum x1, other arithmetic, shards(): score = lax.psum(jnp.sum(power, 2) / F, 'seg')  10.6 us
    reduce_sum x1, other arithmetic, spectra(): jnp.sum(weight * (imag_part[:, :, d] * real_part[:, :, e] - real_part[:,...  6.48 us
  transfers between devices with their start and end apart: 1, of which 1 were waited for; matrix products, arithmetic and copies ran while one was open for 8% of the time, Pallas kernels for 0%

commit v1 on v0

v1 whole, which is shorter than its diff:
```python
import math

import jax
import jax.numpy as jnp
from jax import lax
from jax.experimental import pallas as pl
from jax.experimental.pallas import tpu as pltpu
from jax.sharding import PartitionSpec as P

LANES = 128
FAN = 4
MIB = 1 << 20


def sincos(x):
    turns = jnp.floor(x * (2.0 / math.pi) + 0.5)
    r = x - turns * 1.5703125
    r = r - turns * 4.837512969970703125e-4
    r = r - turns * 7.54978995489188216e-8
    z = r * r
    s = r + r * z * (-1.6666654611e-1 + z * (8.3321608736e-3 + z * (-1.9515295891e-4)))
    c = 1.0 - 0.5 * z + z * z * (4.166664568298827e-2 + z * (-1.388731625493765e-3 + z * 2.443315711809948e-5))
    q = turns.astype(jnp.int32)
    swap = (q & 1) == 1
    sin = jnp.where(swap, c, s)
    cos = jnp.where(swap, s, c)
    sin = jnp.where((q & 2) == 2, -sin, sin)
    cos = jnp.where(((q + 1) & 2) == 2, -cos, cos)
    return sin, cos


def times(a, b):
    return a[0] * b[0] - a[1] * b[1], a[1] * b[0] + a[0] * b[1]


def hi_lo(x):
    hi = x.astype(jnp.bfloat16)
    return hi, (x - hi.astype(jnp.float32)).astype(jnp.bfloat16)


def direction_rows(ids_refs, patterns, delays, grid_points):
    picked = []
    for ref in ids_refs:
        for row in range(ref.shape[0]):
            ids = ref[row : row + 1, :]
            page = jnp.broadcast_to(ids >> 7, (8, LANES))
            lane = jnp.broadcast_to(ids & 127, (8, LANES))
            first = jnp.zeros((8, LANES), jnp.float32)
            second = first
            for h in range(grid_points // LANES):
                here = page == h
                cut = slice(h * LANES, (h + 1) * LANES)
                first = jnp.where(here, jnp.take_along_axis(patterns[:, cut], lane, axis=1), first)
                second = jnp.where(here, jnp.take_along_axis(delays[:, cut], lane, axis=1), second)
            picked.append((first, second))
    first = jnp.concatenate([a for a, _ in picked], 1)
    second = jnp.concatenate([b for _, b in picked], 1)
    plus = [first[d : d + 1] for d in range(3)]
    cross = [first[d : d + 1] for d in range(3, 6)]
    null = [
        plus[1] * cross[2] - plus[2] * cross[1],
        plus[2] * cross[0] - plus[0] * cross[2],
        plus[0] * cross[1] - plus[1] * cross[0],
    ]
    norm2 = jnp.maximum(null[0] * null[0] + null[1] * null[1] + null[2] * null[2], 0.25)
    lag = [second[0:1] - second[1:2], second[1:2] - second[2:3]]
    squares = [n * n / norm2 for n in null]
    pairs = [2.0 * null[0] * null[1] / norm2, 2.0 * null[0] * null[2] / norm2, 2.0 * null[1] * null[2] / norm2]
    return lag, pairs, squares


def front_kernel(cfg, strain, flags, ids_a, ids_b, grid_patterns, grid_delays, *rest):
    n, share, width, ndir, bins = cfg["n"], cfg["share"], cfg["width"], cfg["ndir"], cfg["bins"]
    outs, rows_out = rest[:FAN], rest[FAN]
    tables, held, patterns, delays, sems, table_sem = rest[FAN + 1 :]
    segs = strain.shape[0]
    me = lax.axis_index("seg")
    base = lax.axis_index("dir") * width if cfg["split"] > 1 else 0
    blocks = n // FAN

    copies = [
        pltpu.make_async_copy(grid_patterns, patterns.at[0:6], table_sem.at[0]),
        pltpu.make_async_copy(grid_delays, delays.at[0:3], table_sem.at[1]),
    ]
    for copy in copies:
        copy.start()
    reads = []
    for t in range(n):
        start = pl.multiple_of((me ^ t) * share + base, LANES)
        reads.append(pltpu.make_async_copy(strain.at[:, :, :, pl.ds(start, width)], held.at[t], sems.at[t]))
        reads[-1].start()
    for copy in copies:
        copy.wait()

    ids = [ids_a] if ids_b is None else [ids_a, ids_b]
    lag, pairs, squares = direction_rows(ids, patterns, delays, grid_patterns.shape[1])
    turn = 2.0 * math.pi / bins
    rows_out[...] = jnp.concatenate([lag[0], lag[1], *pairs, *squares], 0)

    low = lax.broadcasted_iota(jnp.int32, (8, ndir), 0).astype(jnp.float32) * turn
    grown = []
    for p in range(2):
        s, c = sincos(lag[p] * low)
        c_all, s_all = c, s
        size = 8
        while size < width:
            sj, cj = sincos(lag[p] * (size * turn))
            cn, sn = times((c_all, s_all), (cj, sj))
            c_all, s_all = jnp.concatenate([c_all, cn], 0), jnp.concatenate([s_all, sn], 0)
            size *= 2
        grown.append((c_all, s_all))
    at = [grown[0], times(grown[0], grown[1]), grown[1]]
    for p in range(3):
        for half in range(2):
            hi, lo = hi_lo(at[p][half])
            tables[p, 0, half * width : (half + 1) * width] = hi
            tables[p, 1, half * width : (half + 1) * width] = lo

    first_bin = ((lax.broadcasted_iota(jnp.int32, (n, ndir), 0) ^ me) * share + base).astype(jnp.float32) * turn
    far = []
    for p in range(2):
        s, c = sincos(lag[p] * first_bin)
        far.append((c, s))
    far = [far[0], times(far[0], far[1]), far[1]]

    weight = flags[...].astype(jnp.float32)
    masks = [jnp.broadcast_to(weight[:, s : s + 1], (8, width)) for s in range(segs)]
    totals = [jnp.zeros((8, width), jnp.float32) for _ in range(3)]
    for t in range(n):
        reads[t].wait()
        out, q = outs[t % FAN], (t // FAN) * 9
        acc = [jnp.zeros((8, width), jnp.float32) for _ in range(9)]
        for s in range(segs):
            x = [held[t, s, c] for c in range(6)]
            y = [masks[s] * v for v in x]
            for d in range(3):
                acc[d] = acc[d] + (y[d] * x[d] + y[d + 3] * x[d + 3])
            for i, (d, e) in enumerate(((0, 1), (0, 2), (1, 2))):
                acc[3 + i] = acc[3 + i] + (y[d] * x[e] + y[d + 3] * x[e + 3])
                acc[6 + i] = acc[6 + i] + (y[d + 3] * x[e] - y[d] * x[e + 3])
        for c in range(9):
            out[q + c] = acc[c]
        for d in range(3):
            totals[d] = totals[d] + acc[d]

    score = jnp.zeros((8, ndir), jnp.float32)
    for d in range(3):
        score = score + jnp.sum(totals[d], 1, keepdims=True) * squares[d]
    for p in range(3):
        real = jnp.concatenate([outs[t % FAN][(t // FAN) * 9 + 3 + p] for t in range(n)], 0)
        imag = jnp.concatenate([outs[t % FAN][(t // FAN) * 9 + 6 + p] for t in range(n)], 0)
        left = jnp.concatenate([jnp.concatenate([real, imag], 1), jnp.concatenate([imag, -real], 1)], 0)
        hi, lo = hi_lo(left)
        dot = lambda a, b: jnp.dot(a, b, preferred_element_type=jnp.float32)
        both = dot(hi, tables[p, 0]) + dot(lo, tables[p, 0]) + dot(hi, tables[p, 1])
        part = jnp.zeros((8, ndir), jnp.float32)
        for t in range(n):
            part = part + far[p][0][t : t + 1] * both[t * 8 : t * 8 + 8]
            part = part + far[p][1][t : t + 1] * both[(n + t) * 8 : (n + t) * 8 + 8]
        score = score + pairs[p] * part
    score = score * (1.0 / bins)
    count = jnp.broadcast_to(jnp.sum(weight, 1, keepdims=True), (8, width))
    for out in outs:
        for i in range(ndir // width):
            out[blocks * 9 + i] = score[:, i * width : (i + 1) * width]
        out[blocks * 9 + ndir // width] = count


def merge_kernel(blocks, extra, *refs):
    ins, outs = refs[:FAN], refs[FAN:]
    add = lambda i: (ins[0][i] + ins[1][i]) + (ins[2][i] + ins[3][i])
    for b in range(blocks):
        for c in range(9):
            outs[b % FAN][(b // FAN) * 9 + c] = add(b * 9 + c)
    for i in range(extra):
        tail = add(blocks * 9 + i)
        for out in outs:
            out[(blocks // FAN) * 9 + i] = tail


def factor_kernel(cfg, rows, *outs):
    share, width, ndir, bins = cfg["share"], cfg["width"], cfg["ndir"], cfg["bins"]
    factors, squares = outs
    first = lax.axis_index("seg") * share + (lax.axis_index("dir") * width if cfg["split"] > 1 else 0)
    freq = (lax.broadcasted_iota(jnp.int32, (1, width), 1) + first).astype(jnp.float32) * (2.0 * math.pi / bins)
    step = LANES
    for k in range(0, ndir, step):
        cols = jnp.transpose(rows[:, k : k + step], (1, 0))
        col = lambda i, w: jnp.broadcast_to(cols[:, i : i + 1], (step, w))
        here = []
        for p in range(2):
            s, c = sincos(col(p, width) * freq)
            here.append((c, s))
        here = [here[0], times(here[0], here[1]), here[1]]
        for p in range(3):
            scale = col(2 + p, width)
            factors[p, k : k + step] = scale * here[p][0]
            factors[3 + p, k : k + step] = scale * here[p][1]
        for d in range(3):
            squares[d, k : k + step] = col(5 + d, LANES)


def project_kernel(cfg, *refs):
    width, ndir = cfg["width"], cfg["ndir"]
    ins, (factors, squares), (keep, send), (spread,) = refs[:FAN], refs[FAN : FAN + 2], refs[FAN + 2 : FAN + 4], refs[FAN + 4 :]
    add = lambda i: (ins[0][i] + ins[1][i]) + (ins[2][i] + ins[3][i])
    scale = 1.0 / jnp.maximum(add(9 + ndir // width), 1.0)
    step = 16
    for f in range(0, width, LANES):
        lanes = slice(f, f + LANES)
        for c in range(9):
            cov = add(c)[:, lanes]
            for w in range(8):
                spread[c, w] = jnp.broadcast_to(cov[w : w + 1], (8, LANES))

        def body(i, best):
            k = pl.multiple_of(i * step, step)
            best = list(best)
            for j in range(0, step, 8):
                a = [squares[d, pl.ds(k + j, 8)] for d in range(3)]
                a += [factors[c, pl.ds(k + j, 8), lanes] for c in range(6)]
                for w in range(8):
                    terms = [a[c] * spread[c, w] for c in range(9)]
                    while len(terms) > 1:
                        terms = [terms[m] + terms[m + 1] if m + 1 < len(terms) else terms[m] for m in range(0, len(terms), 2)]
                    best[w] = jnp.maximum(best[w], terms[0])
            return tuple(best)

        low = jnp.full((8, LANES), -jnp.inf, jnp.float32)
        best = lax.fori_loop(0, ndir // step, body, (low,) * 8)
        peak = jnp.concatenate([jnp.max(b, 0, keepdims=True) for b in best], 0) * scale[:, lanes]
        keep[:, lanes] = peak
        send[:, lanes] = peak
    half = ndir // width // cfg["split"]
    for i in range(half):
        keep[:, (1 + i) * width : (2 + i) * width] = add(9 + i) * scale
        if cfg["split"] > 1:
            send[:, (1 + i) * width : (2 + i) * width] = add(9 + half + i) * scale


def finish_kernel(cfg, keep, other, peak, score):
    width, split = cfg["width"], cfg["split"]
    if split > 1:
        core = lax.axis_index("dir")
        peak[:, pl.ds(pl.multiple_of(core * width, LANES), width)] = keep[:, :width]
        peak[:, pl.ds(pl.multiple_of((1 - core) * width, LANES), width)] = other[:, :width]
        score[...] = keep[:, width:] + other[:, width:]
    else:
        peak[...] = jnp.maximum(keep[:, :width], other[:, :width])
        score[...] = keep[:, width:]


def call(kernel, out_shape, in_spaces, vmem, scratch=(), flops=0, nbytes=0, name=None):
    spec = {"v": pltpu.VMEM, "a": pl.ANY}
    return pl.pallas_call(
        kernel,
        out_shape=out_shape,
        in_specs=[pl.BlockSpec(memory_space=spec[s]) for s in in_spaces],
        out_specs=jax.tree.map(lambda _: pl.BlockSpec(memory_space=pltpu.VMEM), out_shape),
        scratch_shapes=scratch,
        compiler_params=pltpu.CompilerParams(vmem_limit_bytes=vmem * MIB),
        cost_estimate=pl.CostEstimate(flops=flops, bytes_accessed=nbytes, transcendentals=0),
        name=name,
    )


def shards(strain, valid_flags, direction_ids, grid_patterns, grid_delays):
    n, pair = lax.axis_size("seg"), lax.axis_size("dir")
    segs, windows, _, bins = strain.shape
    grid_points = grid_patterns.shape[0]
    share = bins // n
    split = pair if share % (pair * LANES) == 0 else 1
    width = share // split
    own = direction_ids.shape[0]
    ndir = own * split
    cfg = dict(n=n, share=share, split=split, width=width, ndir=ndir, bins=bins)
    f32 = lambda *shape: jax.ShapeDtypeStruct(shape, jnp.float32)
    swap = [(i, i ^ 1) for i in range(pair)]

    ids = direction_ids.reshape(own // LANES, LANES)
    lists = [ids] + ([lax.ppermute(ids, "dir", swap)] if split > 1 else [])
    extra = ndir // width + 1
    blocks = n // FAN

    def front(*refs):
        if split > 1:
            front_kernel(cfg, *refs)
        else:
            front_kernel(cfg, *refs[:3], None, *refs[3:])

    *parts, rows = call(
        front,
        [f32(blocks * 9 + extra, 8, width)] * FAN + [f32(8, ndir)],
        "av" + "v" * len(lists) + "aa",
        40,
        [
            pltpu.VMEM((3, 2, 2 * width, ndir), jnp.bfloat16),
            pltpu.VMEM((n, segs, 6, windows, width), jnp.float32),
            pltpu.VMEM((8, grid_points), jnp.float32),
            pltpu.VMEM((8, grid_points), jnp.float32),
            pltpu.SemaphoreType.DMA((n,)),
            pltpu.SemaphoreType.DMA((2,)),
        ],
        name="front",
    )(jnp.transpose(strain, (0, 2, 1, 3)), valid_flags.T, *lists, grid_patterns.T, grid_delays.T)

    factors, squares = call(
        lambda *refs: factor_kernel(cfg, *refs),
        [f32(6, ndir, width), f32(3, ndir, LANES)],
        "v",
        20,
        flops=ndir * width * 60,
        nbytes=ndir * width * 24,
        name="factors",
    )(rows)

    offset = 1
    while True:
        seen = [parts[0]]
        for r in range(1, FAN):
            seen.append(lax.ppermute(parts[r], "seg", [(i, i ^ (r * offset)) for i in range(n)]))
        offset *= FAN
        if blocks == 1:
            break
        parts = call(
            lambda *refs: merge_kernel(blocks, extra, *refs),
            [f32(blocks // FAN * 9 + extra, 8, width)] * FAN,
            "vvvv",
            8,
            name="merge",
        )(*seen)
        blocks //= FAN

    keep, send = call(
        lambda *refs: project_kernel(cfg, *refs),
        [f32(8, width + own), f32(8, width + own if split > 1 else width)],
        "vvvvvv",
        20,
        [pltpu.VMEM((9, 8, 8, LANES), jnp.float32)],
        name="project",
    )(*seen, factors, squares)
    other = lax.ppermute(send, "dir", swap)
    return tuple(
        call(
            lambda *refs: finish_kernel(cfg, *refs),
            [f32(8, share), f32(8, own)],
            "vv",
            2,
            name="finish",
        )(keep, other)
    )


def solution(mesh):
    placed = (P("seg", None, None, None), P("seg", None), P("dir"), P(), P())
    return jax.shard_map(
        shards,
        mesh=mesh,
        in_specs=placed,
        out_specs=(P(None, "seg"), P(None, "dir")),
        check_vma=False,
    )
```

time: 200 us -> 57.6 us (0.29)
  blocking collectives: 123 us -> 0 us
  other arithmetic: 30.5 us -> 0 us
  Pallas kernels: 0 us -> 18.1 us
  between operations: 14.2 us -> 0.68 us
  starting transfers between devices: 0.04 us -> 9.5 us
  local copies, waits for them, and re-layouts: 3.19 us -> 7.7 us
  waiting for transfers between devices: 25.3 us -> 21.3 us
  matrix products: 2.97 us -> 0 us
    psum x2 -> x0, blocking collectives: 119 us -> none  [the longest x1 75.6 us: shards(): score = lax.psum(jnp.sum(power, 2) / F, 'seg')]
    reduce_scatter x1 -> x0, waiting for transfers between devices: 25.3 us -> none  [shards(): lax.psum_scatter(spectra(strain, valid_flags), 'seg', scatter_dimension=2...]
    ppermute x0 -> x8, waiting for transfers between devices: none -> 21.3 us  [the longest x6 19.9 us: shards(): lax.ppermute(parts[r], 'seg', [(i, i ^ r * offset) for i in range(n)])]
    pallas_call x0 -> x5, Pallas kernels: none -> 18.1 us  [the longest x1 7.3 us: shards(): call(front, [f32(blocks * 9 + extra, 8, width)] * FAN + [f32(8, ndir)], '...]
    reduce_sum x4 -> x0, other arithmetic: 17.1 us -> none  [the longest x1 10.6 us: shards(): score = lax.psum(jnp.sum(power, 2) / F, 'seg')]
    cos x1 -> x0, other arithmetic: 12.5 us -> none  [project(): jnp.cos(angle)[:, None, :] * cov[3 + index][None]]
    ppermute x0 -> x8, starting transfers between devices: none -> 9.5 us  [the longest x6 8.87 us: shards(): lax.ppermute(parts[r], 'seg', [(i, i ^ r * offset) for i in range(n)])]
    unnamed x19 -> x9, local copies, waits for them, and re-layouts: 2.3 us -> 7.7 us
  transfers between devices with their start and end apart: 1 -> 8, of which waited for: 1 -> 5; matrix products, arithmetic and copies ran while one was open for 8% -> 1% of each run, Pallas kernels for 0% -> 6%
where the time goes in v1:
time: 57.6 us; the launch traced here: 57.3 us
  waiting for transfers between devices  21.3 us (37%)
  Pallas kernels  18.1 us (31%)
  starting transfers between devices  9.5 us (16%)
  local copies, waits for them, and re-layouts  7.7 us (13%)
  between operations  0.68 us (1%)
    ppermute x6, waiting for transfers between devices, shards(): lax.ppermute(parts[r], 'seg', [(i, i ^ r * offset) for i in range(n)])  19.9 us
    ppermute x6, starting transfers between devices, shards(): lax.ppermute(parts[r], 'seg', [(i, i ^ r * offset) for i in range(n)])  8.87 us
    unnamed x9, local copies, waits for them, and re-layouts  7.7 us
    pallas_call x1, Pallas kernels, shards(): call(front, [f32(blocks * 9 + extra, 8, width)] * FAN + [f32(8, ndir)], '...  7.3 us
    pallas_call x1, Pallas kernels, shards(): call(lambda *refs: project_kernel(cfg, *refs), [f32(8, width + own), f32(...  6.52 us
    pallas_call x1, Pallas kernels, shards(): call(lambda *refs: factor_kernel(cfg, *refs), [f32(6, ndir, width), f32(3...  3.59 us
    ppermute x1, waiting for transfers between devices, shards(): other = lax.ppermute(send, 'dir', swap)  1.18 us
  transfers between devices with their start and end apart: 8, of which 5 were waited for; matrix products, arithmetic and copies ran while one was open for 1% of the time, Pallas kernels for 6%

profile of v1, /device:TPU:0, one launch (start us, length us, event | category | flops | bytes accessed | tf_op | source)
XLA Modules:
  0.0 57.3 jit_solution(9943625723742472086)
XLA Ops:
  0.6 0.6 collective-permute-start
  1.2 0.8 %copy.7 = s32[8,8]{0,1:T(8,128)S(1)} copy(s32[8,8]{1,0:T(8,128)} %param.6) | data formatting | bytes 512 | tf_op args[1]
  1.9 0.3 collective-permute-done.refs_3_
  2.2 0.0 copy-start
  2.2 4.6 %copy-done = f32[8,8,6,8192]{3,1,2,0:T(8,128)S(1)} copy-done((f32[8,8,6,8192]{3,1,2,0:T(8,128)S(1)}, f32[8,8,6,8192]{3,1,2,0:T(8,128)}, u32[]{:S(2)}) %copy-start) | copy-done | bytes 12582936
  6.8 0.0 copy-start.1
  6.8 0.9 %copy-done.1 = f32[3072,6]{0,1:T(8,128)S(1)} copy-done((f32[3072,6]{0,1:T(8,128)S(1)}, f32[3072,6]{0,1:T(8,128)}, u32[]{:S(2)}) %copy-start.1) | copy-done | bytes 73752
  7.7 0.0 copy-start.2
  7.7 0.8 %copy-done.2 = f32[3072,3]{0,1:T(4,128)S(1)} copy-done((f32[3072,3]{0,1:T(4,128)S(1)}, f32[3072,3]{0,1:T(4,128)}, u32[]{:S(2)}) %copy-start.2) | copy-done | bytes 36888
  8.5 0.0 copy-start.3
  8.5 0.7 %copy-done.3 = s32[512]{0:T(512)S(1)} copy-done((s32[512]{0:T(512)S(1)}, s32[512]{0:T(512)}, u32[]{:S(2)}) %copy-start.3) | copy-done | bytes 2072
  9.2 7.3 %front.1 = (f32[41,8,256]{2,1,0:T(8,128)S(1)}, f32[41,8,256]{2,1,0:T(8,128)S(1)}, f32[41,8,256]{2,1,0:T(8,128)S(1)}, f32[41,8,256]{2,1,0:T(8,128)S(1)}, f32[8,1024]{1,0:T(8,128)S(1)}) custom-call(f32[8,6,8,8192]{3,2,1,0:T(8,128)S(1)} %bitcast.5, s32[8,8]{1,0:T(8,128)S(1)} %bitcast.8, s32[4,128]{1,0:T(4,128)S(1)} %bitcast.10, ...), custom_call_target="tpu_custom_call" | custom-call | tf_op jit(solution)/shard_map/front/pallas_call | solution.py:291
  16.5 2.9 %collective-permute-start.1 = (f32[41,8,256]{2,1,0:T(8,128)S(1)}, f32[41,8,256]{2,1,0:T(8,128)S(1)}, u32[]{:S(2)}, u32[]{:S(2)}) collective-permute-start(f32[41,8,256]{2,1,0:T(8,128)S(1)} %get-tuple-element.16), channel_id=1, source_target_pairs={{0,2},{2,0},{4,6},{6,4},{8,10},{10,8},{12,14},{14,12},{16,18},{18,... | collective-permute-start | bytes 1007624 | tf_op jit(solution)/shard_map/ppermute | solution.py:321
  19.4 1.5 %collective-permute-start.2 = (f32[41,8,256]{2,1,0:T(8,128)S(1)}, f32[41,8,256]{2,1,0:T(8,128)S(1)}, u32[]{:S(2)}, u32[]{:S(2)}) collective-permute-start(f32[41,8,256]{2,1,0:T(8,128)S(1)} %get-tuple-element.17), channel_id=1, source_target_pairs={{0,4},{2,6},{4,0},{6,2},{8,12},{10,14},{12,8},{14,10},{16,20},{18,... | collective-permute-start | bytes 1007624 | tf_op jit(solution)/shard_map/ppermute | solution.py:321
  20.9 0.0 collective-permute-start.3
  20.9 7.2 %collective-permute-done.1.refs_1_ = f32[41,8,256]{2,1,0:T(8,128)S(1)} collective-permute-done((f32[41,8,256]{2,1,0:T(8,128)S(1)}, f32[41,8,256]{2,1,0:T(8,128)S(1)}, u32[]{:S(2)}, u32[]{:S(2)}) %collective-permute-start.1) | collective-permute-done | bytes 335904 | tf_op jit(solution)/shard_map/ppermute | solution.py:321
  28.1 8.1 %collective-permute-done.2.refs_2_ = f32[41,8,256]{2,1,0:T(8,128)S(1)} collective-permute-done((f32[41,8,256]{2,1,0:T(8,128)S(1)}, f32[41,8,256]{2,1,0:T(8,128)S(1)}, u32[]{:S(2)}, u32[]{:S(2)}) %collective-permute-start.2) | collective-permute-done | bytes 335904 | tf_op jit(solution)/shard_map/ppermute | solution.py:321
  36.2 0.0 collective-permute-done.3.refs_3_
  36.2 0.1 merge.1
  36.3 1.6 %collective-permute-start.4 = (f32[14,8,256]{2,1,0:T(8,128)S(1)}, f32[14,8,256]{2,1,0:T(8,128)S(1)}, u32[]{:S(2)}, u32[]{:S(2)}) collective-permute-start(f32[14,8,256]{2,1,0:T(8,128)S(1)} %get-tuple-element.20), channel_id=1, source_target_pairs={{0,8},{2,10},{4,12},{6,14},{8,0},{10,2},{12,4},{14,6},{16,24},{18,... | collective-permute-start | bytes 344072 | tf_op jit(solution)/shard_map/ppermute | solution.py:321
  38.0 2.6 %collective-permute-start.5 = (f32[14,8,256]{2,1,0:T(8,128)S(1)}, f32[14,8,256]{2,1,0:T(8,128)S(1)}, u32[]{:S(2)}, u32[]{:S(2)}) collective-permute-start(f32[14,8,256]{2,1,0:T(8,128)S(1)} %get-tuple-element.21), channel_id=1, source_target_pairs={{0,16},{2,18},{4,20},{6,22},{8,24},{10,26},{12,28},{14,30},{16,0},... | collective-permute-start | bytes 344072 | tf_op jit(solution)/shard_map/ppermute | solution.py:321
  40.6 0.2 collective-permute-start.6
  40.8 3.6 %factors.1 = (f32[6,1024,256]{2,1,0:T(8,128)S(1)}, f32[3,1024,128]{2,1,0:T(8,128)S(1)}) custom-call(f32[8,1024]{1,0:T(8,128)S(1)} %get-tuple-element.23.refs_0_), custom_call_target="tpu_custom_call" | custom-call | flops 15728640 | bytes 6291456 | tf_op jit(solution)/shard_map/factors/pallas_call | solution.py:307
  44.4 0.0 collective-permute-done.4.refs_1_
  44.4 4.5 %collective-permute-done.5.refs_2_ = f32[14,8,256]{2,1,0:T(8,128)S(1)} collective-permute-done((f32[14,8,256]{2,1,0:T(8,128)S(1)}, f32[14,8,256]{2,1,0:T(8,128)S(1)}, u32[]{:S(2)}, u32[]{:S(2)}) %collective-permute-start.5) | collective-permute-done | bytes 114720 | tf_op jit(solution)/shard_map/ppermute | solution.py:321
  48.9 0.0 collective-permute-done.6.refs_3_
  48.9 6.5 %project.1 = (f32[8,768]{1,0:T(8,128)S(1)}, f32[8,768]{1,0:T(8,128)S(1)}) custom-call(f32[14,8,256]{2,1,0:T(8,128)S(1)} %get-tuple-element.19.refs_0_, f32[14,8,256]{2,1,0:T(8,128)S(1)} %collective-permute-done.4.refs_1_, f32[14,8,256]{2,1,0:T(8,128)S(1)} %collective-permute-done.5.refs_2_, f32[14,8,256]{2,1,0:T(8,128)S(1)} %collective-permute-done.6.refs_3_, ...), custom_call_target="tpu_custom_call" | custom-call | tf_op jit(solution)/shard_map/project/pallas_call | solution.py:334
  55.5 0.1 collective-permute-start.7
  55.5 1.2 %collective-permute-done.7.refs_1_ = f32[8,768]{1,0:T(8,128)S(1)} collective-permute-done((f32[8,768]{1,0:T(8,128)S(1)}, f32[8,768]{1,0:T(8,128)S(1)}, u32[]{:S(2)}, u32[]{:S(2)}) %collective-permute-start.7) | collective-permute-done | bytes 24608 | tf_op jit(solution)/shard_map/ppermute | solution.py:342
  56.7 0.6 %finish.1 = (f32[8,512]{1,0:T(8,128)}, f32[8,512]{1,0:T(8,128)}) custom-call(f32[8,768]{1,0:T(8,128)S(1)} %get-tuple-element.26.refs_0_, f32[8,768]{1,0:T(8,128)S(1)} %collective-permute-done.7.refs_1_), custom_call_target="tpu_custom_call" | custom-call | tf_op jit(solution)/shard_map/finish/pallas_call | solution.py:344
Async XLA Ops:
  0.6 1.6 %collective-permute-start = (s32[4,128]{1,0:T(4,128)}, s32[4,128]{1,0:T(4,128)S(1)}, u32[]{:S(2)}, u32[]{:S(2)}) collective-permute-start(s32[4,128]{1,0:T(4,128)} %bitcast.9), channel_id=1, source_target_pairs={{0,1},{1,0},{2,3},{3,2},{4,5},{5,4},{6,7},{7,6},{8,9},{9,8},{10,11... | collective-permute-start | bytes 6152 | tf_op jit(solution)/shard_map/ppermute | solution.py:281
  2.2 4.6 %copy-start = (f32[8,8,6,8192]{3,1,2,0:T(8,128)S(1)}, f32[8,8,6,8192]{3,1,2,0:T(8,128)}, u32[]{:S(2)}) copy-start(f32[8,8,6,8192]{3,1,2,0:T(8,128)} %param.5) | copy-start | bytes 37748740
  6.8 0.9 %copy-start.1 = (f32[3072,6]{0,1:T(8,128)S(1)}, f32[3072,6]{0,1:T(8,128)}, u32[]{:S(2)}) copy-start(f32[3072,6]{0,1:T(8,128)} %param.8) | copy-start | bytes 221188
  7.7 0.8 %copy-start.2 = (f32[3072,3]{0,1:T(4,128)S(1)}, f32[3072,3]{0,1:T(4,128)}, u32[]{:S(2)}) copy-start(f32[3072,3]{0,1:T(4,128)} %param.9) | copy-start | bytes 110596
  8.5 0.7 %copy-start.3 = (s32[512]{0:T(512)S(1)}, s32[512]{0:T(512)}, u32[]{:S(2)}) copy-start(s32[512]{0:T(512)} %param.7) | copy-start | bytes 6148
  16.5 11.6 %collective-permute-start.1 = (f32[41,8,256]{2,1,0:T(8,128)S(1)}, f32[41,8,256]{2,1,0:T(8,128)S(1)}, u32[]{:S(2)}, u32[]{:S(2)}) collective-permute-start(f32[41,8,256]{2,1,0:T(8,128)S(1)} %get-tuple-element.16), channel_id=1, source_target_pairs={{0,2},{2,0},{4,6},{6,4},{8,10},{10,8},{12,14},{14,12},{16,18},{18,... | collective-permute-start | bytes 1007624 | tf_op jit(solution)/shard_map/ppermute | solution.py:321
  19.4 16.9 %collective-permute-start.2 = (f32[41,8,256]{2,1,0:T(8,128)S(1)}, f32[41,8,256]{2,1,0:T(8,128)S(1)}, u32[]{:S(2)}, u32[]{:S(2)}) collective-permute-start(f32[41,8,256]{2,1,0:T(8,128)S(1)} %get-tuple-element.17), channel_id=1, source_target_pairs={{0,4},{2,6},{4,0},{6,2},{8,12},{10,14},{12,8},{14,10},{16,20},{18,... | collective-permute-start | bytes 1007624 | tf_op jit(solution)/shard_map/ppermute | solution.py:321
  20.9 15.4 %collective-permute-start.3 = (f32[41,8,256]{2,1,0:T(8,128)S(1)}, f32[41,8,256]{2,1,0:T(8,128)S(1)}, u32[]{:S(2)}, u32[]{:S(2)}) collective-permute-start(f32[41,8,256]{2,1,0:T(8,128)S(1)} %get-tuple-element.18), channel_id=1, source_target_pairs={{0,6},{2,4},{4,2},{6,0},{8,14},{10,12},{12,10},{14,8},{16,22},{18,... | collective-permute-start | bytes 1007624 | tf_op jit(solution)/shard_map/ppermute | solution.py:321
  36.3 8.1 %collective-permute-start.4 = (f32[14,8,256]{2,1,0:T(8,128)S(1)}, f32[14,8,256]{2,1,0:T(8,128)S(1)}, u32[]{:S(2)}, u32[]{:S(2)}) collective-permute-start(f32[14,8,256]{2,1,0:T(8,128)S(1)} %get-tuple-element.20), channel_id=1, source_target_pairs={{0,8},{2,10},{4,12},{6,14},{8,0},{10,2},{12,4},{14,6},{16,24},{18,... | collective-permute-start | bytes 344072 | tf_op jit(solution)/shard_map/ppermute | solution.py:321
  38.0 11.0 %collective-permute-start.5 = (f32[14,8,256]{2,1,0:T(8,128)S(1)}, f32[14,8,256]{2,1,0:T(8,128)S(1)}, u32[]{:S(2)}, u32[]{:S(2)}) collective-permute-start(f32[14,8,256]{2,1,0:T(8,128)S(1)} %get-tuple-element.21), channel_id=1, source_target_pairs={{0,16},{2,18},{4,20},{6,22},{8,24},{10,26},{12,28},{14,30},{16,0},... | collective-permute-start | bytes 344072 | tf_op jit(solution)/shard_map/ppermute | solution.py:321
  40.6 8.4 %collective-permute-start.6 = (f32[14,8,256]{2,1,0:T(8,128)S(1)}, f32[14,8,256]{2,1,0:T(8,128)S(1)}, u32[]{:S(2)}, u32[]{:S(2)}) collective-permute-start(f32[14,8,256]{2,1,0:T(8,128)S(1)} %get-tuple-element.22), channel_id=1, source_target_pairs={{0,24},{2,26},{4,28},{6,30},{8,16},{10,18},{12,20},{14,22},{16,8},... | collective-permute-start | bytes 344072 | tf_op jit(solution)/shard_map/ppermute | solution.py:321
  55.5 1.3 %collective-permute-start.7 = (f32[8,768]{1,0:T(8,128)S(1)}, f32[8,768]{1,0:T(8,128)S(1)}, u32[]{:S(2)}, u32[]{:S(2)}) collective-permute-start(f32[8,768]{1,0:T(8,128)S(1)} %get-tuple-element.27), channel_id=1, source_target_pairs={{0,1},{1,0},{2,3},{3,2},{4,5},{5,4},{6,7},{7,6},{8,9},{9,8},{10,11... | collective-permute-start | bytes 73736 | tf_op jit(solution)/shard_map/ppermute | solution.py:342
